TPU v7x, 32 devices: a whole 2x2x4 slice. The times are simulated.
32 devices in a mesh: rows: 8 (over z, y), feat: 4 (over x, core).
Axes of the slice: x: 2, y: 2, z: 4, core: 2. Of those that a mesh axis runs over, the one named last changes fastest.
Arguments:
- features: bfloat16 [16384, 1024], P('rows', 'feat'), may hold values from -6 to 6
- tiles: bfloat16 [5120, 128, 128], P('rows'), may hold values from -0.078125 to 0.078125
- tile_row: int32 [5120], P('rows'), may hold values from 0 to 15, as said below
- tile_panel: int32 [5120], P('rows'), may hold values from 0 to 7
- tile_slot: int32 [5120], P('rows'), may hold values from 0 to 7
- counts: int32 [8], P('rows'), may hold values from 1 to 640, as said below
- need_list: int32 [8, 8, 8], replicated, may hold values from 0 to 15, as said below
- weight: bfloat16 [1024, 1024], replicated, may hold values from -0.1875 to 0.1875
Outputs:
- activations: bfloat16 [16384, 1024], P(('rows', 'feat'))
Inputs may be any that keep to these rules, and one draw needn't show every extreme that they name: need_list[g, p] holds 8 distinct tile rows of panel p. Within a row group the slots name distinct (tile_row, tile_panel, tile_slot) triples. `counts`: some row group lists exactly 640 tiles.
All inputs are finite; a program needn't handle non-finite values.
Results may differ from a plain program's by a relative error of at most 0.0049.
Values may be sent and summed in bfloat16 or wider, within the bound.
No kernel may reach another device: no remote copies, remote signals or barrier semaphores. Data moves between devices by JAX's collectives and lax.ppermute only.
A program may use at most 128 MiB of HBM per device.

v0:
```python
import math

import jax
import jax.numpy as jnp
from jax import lax
from jax.sharding import PartitionSpec as P

TILE = 128
TPP = 16
NEED = 8


def aggregate(source, block_ids, tiles, tile_row, live_slot, shard_width):
    slots = tiles.shape[0]
    per_step = math.gcd(slots, 128)
    steps_count = slots // per_step
    blocks = source.reshape(-1, TILE, shard_width)

    def one_step(total, inputs):
        tile_part, id_part, row_part, live_part = inputs
        fetched = jnp.take(blocks, id_part, axis=0)
        product = jnp.einsum("sij,sjh->sih", tile_part, fetched, preferred_element_type=jnp.float32)
        product = jnp.where(live_part[:, None, None], product, 0.0)
        return (total.at[row_part].add(product), None)

    initial = jnp.zeros((TPP, TILE, shard_width), jnp.float32)
    total, unused = lax.scan(
        one_step,
        initial,
        (
            tiles.reshape(steps_count, per_step, TILE, TILE),
            block_ids.reshape(steps_count, per_step),
            tile_row.reshape(steps_count, per_step),
            live_slot.reshape(steps_count, per_step),
        ),
    )
    return total.reshape(TPP * TILE, shard_width)


def per_device(features, tiles, tile_row, tile_panel, tile_slot, counts, need_list, weight):
    shard_width = features.shape[1]
    groups = lax.axis_size("rows")
    own_group = lax.axis_index("rows")
    live_slot = lax.broadcasted_iota(jnp.int32, tile_row.shape, 0) < counts[0]
    wanted = lax.dynamic_index_in_dim(need_list, own_group, 1, keepdims=False)
    outgoing = jnp.take(features.reshape(TPP, TILE, shard_width), wanted.reshape(-1), axis=0)
    outgoing = outgoing.reshape(groups, NEED * TILE, shard_width)
    arrived = lax.all_to_all(outgoing, "rows", split_axis=0, concat_axis=0, tiled=True)
    source = arrived.reshape(groups * NEED * TILE, shard_width)
    block_ids = tile_panel * NEED + tile_slot
    summed = aggregate(source, block_ids, tiles, tile_row, live_slot, shard_width)
    rounded = summed.astype(jnp.bfloat16)
    rows_full = lax.all_to_all(rounded, "feat", split_axis=0, concat_axis=1, tiled=True)
    mixed = jnp.dot(rows_full, weight, preferred_element_type=jnp.float32)
    return jnp.maximum(mixed, 0.0).astype(jnp.bfloat16)


def solution(mesh):
    return jax.shard_map(
        per_device,
        mesh=mesh,
        in_specs=(
            P("rows", "feat"),
            P("rows", None, None),
            P("rows"),
            P("rows"),
            P("rows"),
            P("rows"),
            P(),
            P(),
        ),
        out_specs=P(("rows", "feat"), None),
        check_vma=False,
    )
```

profile of v0, /device:TPU:0, one launch (start us, length us, event | category | flops | bytes accessed | tf_op | source)
XLA Modules:
  0.0 434.4 jit_solution(14390559520812577620)
XLA Ops:
  0.0 0.9 constant_dynamic-slice_fusion.2
  1.0 0.1 copy.14
  1.2 4.0 gather_fusion.1
  5.2 5.3 %bitcast_select_fusion = bf16[8,1024,256]{2,1,0:T(8,128)(2,1)} fusion(pred[8,1024]{1,0:T(8,128)(4,1)S(1)} %broadcast_bitcast_fusion, bf16[8,1024,256]{2,1,0:T(8,128)(2,1)} %bitcast.55), kind=kLoop, calls=%fused_computation.22 | loop fusion | flops 2097152 | bytes 8396800 | tf_op jit(solution)/shard_map/jit(_take)/select_n | solution.py:46
  10.5 7.4 %all-to-all-start = ((bf16[8,1024,256]{2,1,0:T(8,128)(2,1)}), bf16[8,1024,256]{2,1,0:T(8,128)(2,1)}, u32[]{:S(2)}, u32[]{:S(2)}) async-start(bf16[8,1024,256]{2,1,0:T(8,128)(2,1)} %bitcast_select_fusion), calls=%async_computation | async-start | bytes 8388608 | tf_op jit(solution)/shard_map/all_to_all | solution.py:48
  18.6 92.6 %all-to-all-done = bf16[8,1024,256]{2,1,0:T(8,128)(2,1)} async-done(((bf16[8,1024,256]{2,1,0:T(8,128)(2,1)}), bf16[8,1024,256]{2,1,0:T(8,128)(2,1)}, u32[]{:S(2)}, u32[]{:S(2)}) %all-to-all-start) | async-done | bytes 4194336 | tf_op jit(solution)/shard_map/all_to_all | solution.py:48
  111.2 1.6 broadcast_in_dim.43
  112.8 298.1 %while.10 = (s32[]{:T(128)}, f32[16,128,256]{2,1,0:T(8,128)}, s32[5,128]{1,0:T(8,128)}, pred[5,128]{1,0:T(8,128)(4,1)S(1)}, bf16[5,128,128,128]{3,2,1,0:T(8,128)...) while((s32[]{:T(128)}, f32[16,128,256]{2,1,0:T(8,128)}, s32[5,128]{1,0:T(8,128)}, ...), condition=%wide.region_2.3_spmd, body=%wide.region_0.2_spmd.sunk | while | flops 1086327296 | bytes 96478432 | solution.py:27
  112.8 0.7 fusion.18
  113.5 8.8 %gather_fusion = bf16[128,128,256]{2,1,0:T(8,128)(2,1)} fusion(bf16[64,128,256]{2,1,0:T(8,128)(2,1)} %get-tuple-element.128, s32[1024]{0:T(1024)S(1)} %pad_clamp_fusion.3), kind=kCustom, calls=%fused_computation.clone.1 | custom fusion | bytes 16777728 | tf_op jit(solution)/shard_map/while/body/eval_jaxpr/jit(_take)/gather | solution.py:21
  122.2 12.8 %convolution_select_fusion.2 = f32[128,128,256]{2,1,0:T(8,128)} fusion(bf16[128,128,256]{2,1,0:T(8,128)(2,1)} %gather_fusion, pred[128]{0:T(512)(128)(4,1)S(1)} %compare_and_fusion.3, pred[128]{0:T(512)(128)(4,1)S(1)} %dynamic-slice_bitcast_fusion.2, bf16[5,128,128,128]{3,2,1,0:T(8,128)(2,1)} %get-tuple-element.126, s32[]{:T(128)} %get-tuple-element.114), kind=kOutput, calls=%fused_computation.3.clone.1 | convolution fusion | flops 1082130432 | bytes 29360896 | tf_op jit(solution)/shard_map/while/body/eval_jaxpr/sij,sjh->sih/dot_general | solution.py:22
  135.1 37.1 %scatter_fusion = f32[16,128,256]{2,1,0:T(8,128)} fusion(f32[16,128,256]{2,1,0:T(8,128)} %get-tuple-element.115, s32[128]{0:T(128)S(1)} %get-tuple-element.104, f32[128,128,256]{2,1,0:T(8,128)} %convolution_select_fusion.2), kind=kCustom, calls=%fused_computation.2.clone.1 | custom fusion | flops 4194304 | bytes 50332160 | tf_op jit(solution)/shard_map/while/body/eval_jaxpr/scatter-add | solution.py:24
  172.1 0.7 fusion.18
  172.8 8.8 %gather_fusion = bf16[128,128,256]{2,1,0:T(8,128)(2,1)} fusion(bf16[64,128,256]{2,1,0:T(8,128)(2,1)} %get-tuple-element.128, s32[1024]{0:T(1024)S(1)} %pad_clamp_fusion.3), kind=kCustom, calls=%fused_computation.clone.1 | custom fusion | bytes 16777728 | tf_op jit(solution)/shard_map/while/body/eval_jaxpr/jit(_take)/gather | solution.py:21
  181.6 12.8 %convolution_select_fusion.2 = f32[128,128,256]{2,1,0:T(8,128)} fusion(bf16[128,128,256]{2,1,0:T(8,128)(2,1)} %gather_fusion, pred[128]{0:T(512)(128)(4,1)S(1)} %compare_and_fusion.3, pred[128]{0:T(512)(128)(4,1)S(1)} %dynamic-slice_bitcast_fusion.2, bf16[5,128,128,128]{3,2,1,0:T(8,128)(2,1)} %get-tuple-element.126, s32[]{:T(128)} %get-tuple-element.114), kind=kOutput, calls=%fused_computation.3.clone.1 | convolution fusion | flops 1082130432 | bytes 29360896 | tf_op jit(solution)/shard_map/while/body/eval_jaxpr/sij,sjh->sih/dot_general | solution.py:22
  194.4 37.4 %scatter_fusion = f32[16,128,256]{2,1,0:T(8,128)} fusion(f32[16,128,256]{2,1,0:T(8,128)} %get-tuple-element.115, s32[128]{0:T(128)S(1)} %get-tuple-element.104, f32[128,128,256]{2,1,0:T(8,128)} %convolution_select_fusion.2), kind=kCustom, calls=%fused_computation.2.clone.1 | custom fusion | flops 4194304 | bytes 50332160 | tf_op jit(solution)/shard_map/while/body/eval_jaxpr/scatter-add | solution.py:24
  231.8 0.7 fusion.18
  232.5 8.8 %gather_fusion = bf16[128,128,256]{2,1,0:T(8,128)(2,1)} fusion(bf16[64,128,256]{2,1,0:T(8,128)(2,1)} %get-tuple-element.128, s32[1024]{0:T(1024)S(1)} %pad_clamp_fusion.3), kind=kCustom, calls=%fused_computation.clone.1 | custom fusion | bytes 16777728 | tf_op jit(solution)/shard_map/while/body/eval_jaxpr/jit(_take)/gather | solution.py:21
  241.3 12.8 %convolution_select_fusion.2 = f32[128,128,256]{2,1,0:T(8,128)} fusion(bf16[128,128,256]{2,1,0:T(8,128)(2,1)} %gather_fusion, pred[128]{0:T(512)(128)(4,1)S(1)} %compare_and_fusion.3, pred[128]{0:T(512)(128)(4,1)S(1)} %dynamic-slice_bitcast_fusion.2, bf16[5,128,128,128]{3,2,1,0:T(8,128)(2,1)} %get-tuple-element.126, s32[]{:T(128)} %get-tuple-element.114), kind=kOutput, calls=%fused_computation.3.clone.1 | convolution fusion | flops 1082130432 | bytes 29360896 | tf_op jit(solution)/shard_map/while/body/eval_jaxpr/sij,sjh->sih/dot_general | solution.py:22
  254.1 37.7 %scatter_fusion = f32[16,128,256]{2,1,0:T(8,128)} fusion(f32[16,128,256]{2,1,0:T(8,128)} %get-tuple-element.115, s32[128]{0:T(128)S(1)} %get-tuple-element.104, f32[128,128,256]{2,1,0:T(8,128)} %convolution_select_fusion.2), kind=kCustom, calls=%fused_computation.2.clone.1 | custom fusion | flops 4194304 | bytes 50332160 | tf_op jit(solution)/shard_map/while/body/eval_jaxpr/scatter-add | solution.py:24
  291.8 0.7 fusion.18
  292.5 8.8 %gather_fusion = bf16[128,128,256]{2,1,0:T(8,128)(2,1)} fusion(bf16[64,128,256]{2,1,0:T(8,128)(2,1)} %get-tuple-element.128, s32[1024]{0:T(1024)S(1)} %pad_clamp_fusion.3), kind=kCustom, calls=%fused_computation.clone.1 | custom fusion | bytes 16777728 | tf_op jit(solution)/shard_map/while/body/eval_jaxpr/jit(_take)/gather | solution.py:21
  301.3 12.8 %convolution_select_fusion.2 = f32[128,128,256]{2,1,0:T(8,128)} fusion(bf16[128,128,256]{2,1,0:T(8,128)(2,1)} %gather_fusion, pred[128]{0:T(512)(128)(4,1)S(1)} %compare_and_fusion.3, pred[128]{0:T(512)(128)(4,1)S(1)} %dynamic-slice_bitcast_fusion.2, bf16[5,128,128,128]{3,2,1,0:T(8,128)(2,1)} %get-tuple-element.126, s32[]{:T(128)} %get-tuple-element.114), kind=kOutput, calls=%fused_computation.3.clone.1 | convolution fusion | flops 1082130432 | bytes 29360896 | tf_op jit(solution)/shard_map/while/body/eval_jaxpr/sij,sjh->sih/dot_general | solution.py:22
  314.1 37.2 %scatter_fusion = f32[16,128,256]{2,1,0:T(8,128)} fusion(f32[16,128,256]{2,1,0:T(8,128)} %get-tuple-element.115, s32[128]{0:T(128)S(1)} %get-tuple-element.104, f32[128,128,256]{2,1,0:T(8,128)} %convolution_select_fusion.2), kind=kCustom, calls=%fused_computation.2.clone.1 | custom fusion | flops 4194304 | bytes 50332160 | tf_op jit(solution)/shard_map/while/body/eval_jaxpr/scatter-add | solution.py:24
  351.3 0.7 fusion.18
  352.0 8.8 %gather_fusion = bf16[128,128,256]{2,1,0:T(8,128)(2,1)} fusion(bf16[64,128,256]{2,1,0:T(8,128)(2,1)} %get-tuple-element.128, s32[1024]{0:T(1024)S(1)} %pad_clamp_fusion.3), kind=kCustom, calls=%fused_computation.clone.1 | custom fusion | bytes 16777728 | tf_op jit(solution)/shard_map/while/body/eval_jaxpr/jit(_take)/gather | solution.py:21
  360.8 12.8 %convolution_select_fusion.2 = f32[128,128,256]{2,1,0:T(8,128)} fusion(bf16[128,128,256]{2,1,0:T(8,128)(2,1)} %gather_fusion, pred[128]{0:T(512)(128)(4,1)S(1)} %compare_and_fusion.3, pred[128]{0:T(512)(128)(4,1)S(1)} %dynamic-slice_bitcast_fusion.2, bf16[5,128,128,128]{3,2,1,0:T(8,128)(2,1)} %get-tuple-element.126, s32[]{:T(128)} %get-tuple-element.114), kind=kOutput, calls=%fused_computation.3.clone.1 | convolution fusion | flops 1082130432 | bytes 29360896 | tf_op jit(solution)/shard_map/while/body/eval_jaxpr/sij,sjh->sih/dot_general | solution.py:22
  373.6 37.3 %scatter_fusion = f32[16,128,256]{2,1,0:T(8,128)} fusion(f32[16,128,256]{2,1,0:T(8,128)} %get-tuple-element.115, s32[128]{0:T(128)S(1)} %get-tuple-element.104, f32[128,128,256]{2,1,0:T(8,128)} %convolution_select_fusion.2), kind=kCustom, calls=%fused_computation.2.clone.1 | custom fusion | flops 4194304 | bytes 50332160 | tf_op jit(solution)/shard_map/while/body/eval_jaxpr/scatter-add | solution.py:24
  410.9 1.7 convert_element_type.10
  412.6 17.0 %all_to_all.21 = bf16[4,512,256]{2,1,0:T(8,128)(2,1)S(1)} all-to-all(bf16[4,512,256]{2,1,0:T(8,128)(2,1)S(1)} %bitcast.57), channel_id=1, replica_groups=mesh['rows'=8,'feat'=4] {'feat'}, dimensions={0} | all-to-all | bytes 2097152 | tf_op jit(solution)/shard_map/all_to_all | solution.py:53
  429.6 1.3 copy.15
  430.9 3.5 maximum_convert_fusion
  (28 shorter events, 0.4 us)
Async XLA Ops:
  0.0 430.9 %copy-start = (bf16[1024,1024]{1,0:T(8,128)(2,1)S(1)}, bf16[1024,1024]{1,0:T(8,128)(2,1)}, u32[]{:S(2)}) copy-start(bf16[1024,1024]{1,0:T(8,128)(2,1)} %param.17) | copy-start | bytes 6291460
  10.5 8.1 %copy-start.1 = (s32[640]{0:T(1024)S(1)}, s32[640]{0:T(1024)}, u32[]{:S(2)}) copy-start(s32[640]{0:T(1024)} %param.14) | copy-start | bytes 7684
  10.5 8.1 %copy-start.2 = (s32[640]{0:T(1024)S(1)}, s32[640]{0:T(1024)}, u32[]{:S(2)}) copy-start(s32[640]{0:T(1024)} %param.13) | copy-start | bytes 7684
  10.5 100.7 %all-to-all-start = ((bf16[8,1024,256]{2,1,0:T(8,128)(2,1)}), bf16[8,1024,256]{2,1,0:T(8,128)(2,1)}, u32[]{:S(2)}, u32[]{:S(2)}) async-start(bf16[8,1024,256]{2,1,0:T(8,128)(2,1)} %bitcast_select_fusion), calls=%async_computation | async-start | bytes 8388608 | tf_op jit(solution)/shard_map/all_to_all | solution.py:48
where the time goes:
time: 436 us; the launch traced here: 434 us
  other arithmetic  197 us (45%)
  waiting for transfers between devices  92.6 us (21%)
  matrix products  67.5 us (15%)
  local copies, waits for them, and re-layouts  51.9 us (12%)
  blocking collectives  17 us (4%)
  starting transfers between devices  7.44 us (2%)
    scatter-add x5, other arithmetic, one_step(): return (total.at[row_part].add(product), None)  187 us
    all_to_all x1, waiting for transfers between devices, per_device(): lax.all_to_all(outgoing, 'rows', split_axis=0, concat_axis=0, tiled=True)  92.6 us
    dot_general x5, matrix products, one_step(): jnp.einsum('sij,sjh->sih', tile_part, fetched, preferred_element_type=jnp...  64.1 us
    gather x5, local copies, waits for them, and re-layouts, one_step(): fetched = jnp.take(blocks, id_part, axis=0)  43.8 us
    all_to_all x1, blocking collectives, per_device(): lax.all_to_all(rounded, 'feat', split_axis=0, concat_axis=1, tiled=True)  17 us
  transfers between devices with their start and end apart: 1, of which 1 were waited for; matrix products, arithmetic and copies ran while one was open for 0% of the time, Pallas kernels for 0%

commit v1 on v0

v1 whole, which is shorter than its diff:
```python
import functools

import jax
import jax.numpy as jnp
from jax import lax
from jax.experimental import pallas as pl
from jax.experimental.pallas import tpu as pltpu
from jax.sharding import PartitionSpec as P

TILE = 128
TPP = 16
NEED = 8
PER_PANEL = TPP * NEED
VMEM_LIMIT = 60 * 1024 * 1024


def aggregate_kernel(entries, meta, table, tiles, source, out, dense, feats, count, tile_sem, feat_sem):
    def fetch(entry):
        buf = lax.rem(entry, 2)
        base = meta[entry] * PER_PANEL

        def row_step(row, total):
            for k in range(NEED):
                slot = table[base + row * NEED + k]
                rows = pl.ds(pl.multiple_of(row * TILE, TILE), TILE)
                cols = pl.ds(k * TILE, TILE)

                @pl.when(slot > 0)
                def _():
                    pltpu.make_async_copy(tiles.at[slot - 1], dense.at[buf, rows, cols], tile_sem.at[buf]).start()

                @pl.when(slot == 0)
                def _():
                    dense[buf, rows, cols] = jnp.zeros((TILE, TILE), jnp.bfloat16)

                total = total + jnp.where(slot > 0, 1, 0)
            return total

        count[buf] = lax.fori_loop(0, TPP, row_step, 0)

    copy = pltpu.make_async_copy(source, feats, feat_sem)
    copy.start()
    fetch(0)
    out[...] = jnp.zeros_like(out)
    copy.wait()

    def step(entry, carry):
        buf = lax.rem(entry, 2)

        @pl.when(entry + 1 < entries)
        def _():
            fetch(entry + 1)

        def wait_one(i, c):
            pltpu.make_async_copy(tiles.at[0], dense.at[buf, pl.ds(0, TILE), pl.ds(0, TILE)], tile_sem.at[buf]).wait()
            return c

        lax.fori_loop(0, count[buf], wait_one, 0)
        block = 512

        def part(m, c):
            rows = pl.ds(pl.multiple_of(m * block, block), block)
            out[rows, :] += jnp.dot(dense[buf, rows, :], feats[entry], preferred_element_type=jnp.float32)
            return c

        lax.fori_loop(0, TPP * TILE // block, part, 0)
        return carry

    lax.fori_loop(0, entries, step, 0)


def aggregate(meta, table, tiles, source):
    entries, depth, width = source.shape
    return pl.pallas_call(
        functools.partial(aggregate_kernel, entries),
        out_shape=jax.ShapeDtypeStruct((TPP * TILE, width), jnp.float32),
        in_specs=[
            pl.BlockSpec(memory_space=pltpu.SMEM),
            pl.BlockSpec(memory_space=pltpu.SMEM),
            pl.BlockSpec(memory_space=pl.ANY),
            pl.BlockSpec(memory_space=pl.ANY),
        ],
        out_specs=pl.BlockSpec(memory_space=pltpu.VMEM),
        scratch_shapes=[
            pltpu.VMEM((2, TPP * TILE, depth), jnp.bfloat16),
            pltpu.VMEM((entries, depth, width), jnp.bfloat16),
            pltpu.SMEM((2,), jnp.int32),
            pltpu.SemaphoreType.DMA((2,)),
            pltpu.SemaphoreType.DMA,
        ],
        compiler_params=pltpu.CompilerParams(vmem_limit_bytes=VMEM_LIMIT),
        name="aggregate",
    )(meta, table, tiles, source)


def product_kernel(x, w, out):
    blocks, rows, width = x.shape
    total = jnp.dot(x[0], w[0:width, :], preferred_element_type=jnp.float32)
    for f in range(1, blocks):
        total += jnp.dot(x[f], w[f * width : (f + 1) * width, :], preferred_element_type=jnp.float32)
    out[...] = jnp.maximum(total, 0.0).astype(out.dtype)


def product(x, w):
    blocks, rows, width = x.shape
    depth, cols = w.shape
    step = 256
    return pl.pallas_call(
        product_kernel,
        grid=(cols // step,),
        out_shape=jax.ShapeDtypeStruct((rows, cols), jnp.bfloat16),
        in_specs=[
            pl.BlockSpec((blocks, rows, width), lambda j: (0, 0, 0)),
            pl.BlockSpec((depth, step), lambda j: (0, j)),
        ],
        out_specs=pl.BlockSpec((rows, step), lambda j: (0, j)),
        compiler_params=pltpu.CompilerParams(vmem_limit_bytes=32 * 1024 * 1024),
        name="product",
    )(x, w)


def slot_table(groups, tile_row, tile_panel, tile_slot, counts):
    slots = lax.iota(jnp.int32, tile_row.shape[0])
    key = (tile_panel * TPP + tile_row) * NEED + tile_slot
    key = jnp.where(slots < counts[0], key, -1)
    places = lax.iota(jnp.int32, groups * PER_PANEL)
    return jnp.max(jnp.where(key[None, :] == places[:, None], slots[None, :] + 1, 0), axis=1)


def per_device(features, tiles, tile_row, tile_panel, tile_slot, counts, need_list, weight):
    shard_width = features.shape[1]
    groups = lax.axis_size("rows")
    feat = lax.axis_size("feat")
    own_group = lax.axis_index("rows")
    wanted = lax.dynamic_index_in_dim(need_list, own_group, 1, keepdims=False)
    outgoing = features.reshape(TPP, TILE, shard_width).at[wanted.reshape(-1)].get(mode="promise_in_bounds")
    outgoing = outgoing.reshape(groups, NEED * TILE, shard_width)
    arrived = lax.all_to_all(outgoing, "rows", split_axis=0, concat_axis=0, tiled=True)
    table = slot_table(groups, tile_row, tile_panel, tile_slot, counts)
    summed = aggregate(lax.iota(jnp.int32, groups), table, tiles, arrived)
    rounded = summed.astype(jnp.bfloat16).reshape(feat, -1, shard_width)
    rows_full = lax.all_to_all(rounded, "feat", split_axis=0, concat_axis=0, tiled=True)
    return product(rows_full, weight)


def solution(mesh):
    return jax.shard_map(
        per_device,
        mesh=mesh,
        in_specs=(
            P("rows", "feat"),
            P("rows", None, None),
            P("rows"),
            P("rows"),
            P("rows"),
            P("rows"),
            P(),
            P(),
        ),
        out_specs=P(("rows", "feat"), None),
        check_vma=False,
    )
```

time: 436 us -> 157 us (0.36)
  other arithmetic: 197 us -> 2.88 us
  matrix products: 67.5 us -> 0 us
  local copies, waits for them, and re-layouts: 51.9 us -> 4.56 us
  Pallas kernels: 0 us -> 32.5 us
    scatter-add x5 -> x0, other arithmetic: 187 us -> none  [one_step(): return (total.at[row_part].add(product), None)]
    dot_general x6 -> x0, matrix products: 67.5 us -> none  [the longest x5 64.1 us: one_step(): jnp.einsum('sij,sjh->sih', tile_part, fetched, preferred_element_type=jnp...]
    gather x6 -> x1, local copies, waits for them, and re-layouts: 47.8 us -> 2.79 us  [per_device(): features.reshape(TPP, TILE, shard_width).at[wanted.reshape(-1)]]
    pallas_call x0 -> x2, Pallas kernels: none -> 32.5 us  [the longest x1 29.5 us: aggregate(): pl.pallas_call(functools.partial(aggregate_kernel, entries), out_shape=ja...]
    select_n x7 -> x1, other arithmetic: 8.74 us -> 0.01 us  [per_device(): features.reshape(TPP, TILE, shard_width).at[wanted.reshape(-1)]]
  transfers between devices with their start and end apart: 1 -> 1, of which waited for: 1 -> 1; matrix products, arithmetic and copies ran while one was open for 0% -> 1% of each run, Pallas kernels for 0% -> 0%
where the time goes in v1:
time: 157 us
  waiting for transfers between devices  91.6 us (58%)
  Pallas kernels  32.5 us (21%)
  blocking collectives  17 us (11%)
  starting transfers between devices  7.44 us (5%)
  local copies, waits for them, and re-layouts  4.56 us (3%)
  other arithmetic  2.88 us (2%)
    all_to_all x1, waiting for transfers between devices, per_device(): lax.all_to_all(outgoing, 'rows', split_axis=0, concat_axis=0, tiled=True)  91.6 us
    pallas_call x1, Pallas kernels, aggregate(): pl.pallas_call(functools.partial(aggregate_kernel, entries), out_shape=ja...  29.5 us
    all_to_all x1, blocking collectives, per_device(): lax.all_to_all(rounded, 'feat', split_axis=0, concat_axis=0, tiled=True)  17 us
    all_to_all x1, starting transfers between devices, per_device(): lax.all_to_all(outgoing, 'rows', split_axis=0, concat_axis=0, tiled=True)  7.44 us
  transfers between devices with their start and end apart: 1, of which 1 were waited for; matrix products, arithmetic and copies ran while one was open for 1% of the time, Pallas kernels for 0%

profile of v1, /device:TPU:0, one launch (start us, length us, event | category | flops | bytes accessed | tf_op | source)
XLA Modules:
  0.0 156.6 jit_solution(15442295630350038587)
XLA Ops:
  0.0 0.0 copy-start
  0.0 0.9 dynamic-slice_reduce_fusion
  0.9 0.1 reshape.48
  1.0 0.3 copy-done
  1.2 2.8 %gather_fusion = bf16[64,128,256]{2,1,0:T(8,128)(2,1)} fusion(bf16[16,128,256]{2,1,0:T(8,128)(2,1)S(1)} %bitcast.7, s32[1024]{0:T(1024)S(1)} %pad_clamp_fusion), kind=kCustom, calls=%fused_computation | custom fusion | bytes 8388864 | tf_op jit(solution)/shard_map/gather | solution.py:136
  4.0 0.0 copy-start.2
  4.0 0.0 copy-start.3
  4.0 0.0 copy-start.4
  4.0 7.4 %all-to-all-start = ((bf16[8,1024,256]{2,1,0:T(8,128)(2,1)}), bf16[8,1024,256]{2,1,0:T(8,128)(2,1)}, u32[]{:S(2)}, u32[]{:S(2)}) async-start(bf16[8,1024,256]{2,1,0:T(8,128)(2,1)} %bitcast.8), calls=%async_computation | async-start | bytes 8388608 | tf_op jit(solution)/shard_map/all_to_all | solution.py:138
  12.1 0.0 copy-done.2
  12.1 0.0 copy-done.3
  12.1 0.0 copy-done.4
  12.2 1.0 select_reduce_fusion.table
  13.2 91.6 %all-to-all-done.source = bf16[8,1024,256]{2,1,0:T(8,128)(2,1)} async-done(((bf16[8,1024,256]{2,1,0:T(8,128)(2,1)}), bf16[8,1024,256]{2,1,0:T(8,128)(2,1)}, u32[]{:S(2)}, u32[]{:S(2)}) %all-to-all-start) | async-done | bytes 4194336 | tf_op jit(solution)/shard_map/all_to_all | solution.py:138
  104.8 0.5 iota.14.meta
  105.3 29.5 %aggregate.1 = f32[2048,256]{1,0:T(8,128)} custom-call(s32[8]{0:T(128)} %iota.14.meta, s32[1024]{0:T(1024)} %select_reduce_fusion.table, bf16[640,128,128]{2,1,0:T(8,128)(2,1)} %tiles.1, bf16[8,1024,256]{2,1,0:T(8,128)(2,1)} %all-to-all-done.source), custom_call_target="tpu_custom_call" | custom-call | tf_op jit(solution)/shard_map/aggregate/pallas_call | solution.py:74
  134.8 0.0 copy-start.1
  134.8 1.8 %convert_element_type.3 = bf16[2048,256]{1,0:T(8,128)(2,1)S(1)} convert(f32[2048,256]{1,0:T(8,128)} %aggregate.1) | non-fusion elementwise | flops 524288 | bytes 3145728 | tf_op jit(solution)/shard_map/convert_element_type | solution.py:141
  136.7 17.0 %all_to_all.10.x = bf16[4,512,256]{2,1,0:T(8,128)(2,1)S(1)} all-to-all(bf16[4,512,256]{2,1,0:T(8,128)(2,1)S(1)} %bitcast.9), channel_id=1, replica_groups=mesh['rows'=8,'feat'=4] {'feat'}, dimensions={0} | all-to-all | bytes 2097152 | tf_op jit(solution)/shard_map/all_to_all | solution.py:142
  153.7 0.0 copy-done.1
  153.7 3.0 %product.1 = bf16[512,1024]{1,0:T(8,128)(2,1)} custom-call(bf16[4,512,256]{2,1,0:T(8,128)(2,1)S(1)} %all_to_all.10.x, bf16[1024,1024]{1,0:T(8,128)(2,1)S(1)} %copy-done.1), custom_call_target="tpu_custom_call" | custom-call | tf_op jit(solution)/shard_map/product/pallas_call | solution.py:108
  (3 shorter events, 0.0 us)
Async XLA Ops:
  0.0 1.2 copy-start
  4.0 8.1 %copy-start.2 = (s32[640]{0:T(1024)S(1)}, s32[640]{0:T(1024)}, u32[]{:S(2)}) copy-start(s32[640]{0:T(1024)} %param.12) | copy-start | bytes 7684
  4.0 8.1 %copy-start.3 = (s32[640]{0:T(1024)S(1)}, s32[640]{0:T(1024)}, u32[]{:S(2)}) copy-start(s32[640]{0:T(1024)} %param.10) | copy-start | bytes 7684
  4.0 8.1 %copy-start.4 = (s32[640]{0:T(1024)S(1)}, s32[640]{0:T(1024)}, u32[]{:S(2)}) copy-start(s32[640]{0:T(1024)} %param.11) | copy-start | bytes 7684
  4.0 100.7 %all-to-all-start = ((bf16[8,1024,256]{2,1,0:T(8,128)(2,1)}), bf16[8,1024,256]{2,1,0:T(8,128)(2,1)}, u32[]{:S(2)}, u32[]{:S(2)}) async-start(bf16[8,1024,256]{2,1,0:T(8,128)(2,1)} %bitcast.8), calls=%async_computation | async-start | bytes 8388608 | tf_op jit(solution)/shard_map/all_to_all | solution.py:138
  134.8 18.9 %copy-start.1 = (bf16[1024,1024]{1,0:T(8,128)(2,1)S(1)}, bf16[1024,1024]{1,0:T(8,128)(2,1)}, u32[]{:S(2)}) copy-start(bf16[1024,1024]{1,0:T(8,128)(2,1)} %w.1) | copy-start | bytes 6291460
